TPU v7x, 256 devices: a whole 4x4x8 slice. The times are simulated.
256 devices in a mesh: row: 64 (over x, z, core), col: 4 (over y).
Axes of the slice: x: 4, y: 4, z: 8, core: 2. Of those that a mesh axis runs over, the one named last changes fastest.
Arguments:
- pivot_block: float32 [512, 512], P('row', 'col'), as said below
- pivot_tangent: float32 [512, 512], P('row', 'col'), as said below
- panel_block: float32 [65536, 512], P('row', 'col'), may hold values from -1.5 to 1.5
- panel_tangent: float32 [65536, 512], P('row', 'col'), may hold values from -1.5 to 1.5
- strip_block: float32 [65536, 2048], P('row', 'col'), may hold values from -6 to 6
- strip_tangent: float32 [65536, 2048], P('row', 'col'), may hold values from -6 to 6
Outputs:
- pivot_factor: float32 [512, 512], P('row', 'col')
- pivot_factor_tangent: float32 [512, 512], P('row', 'col')
- panel_factor: float32 [65536, 512], P('row', 'col')
- panel_factor_tangent: float32 [65536, 512], P('row', 'col')
- strip_updated: float32 [65536, 2048], P('row', 'col')
- strip_updated_tangent: float32 [65536, 2048], P('row', 'col')
Inputs may be any that keep to these rules, and one draw needn't show every extreme that they name: `pivot_block`: symmetric positive definite; its smallest eigenvalue is at least 0.05. `pivot_tangent`: symmetric.
All inputs are finite; a program needn't handle non-finite values.
Results may differ from a plain program's by a relative error of at most 0.0003.
Values sent between devices are 32-bit elements; how exact they have to be, the bound alone decides.
No kernel may reach another device: no remote copies, remote signals or barrier semaphores. Data moves between devices by JAX's collectives and lax.ppermute only.
A program may use at most 128 MiB of HBM per device.

v0:
```python
import jax
import jax.numpy as jnp
from jax import lax
from jax.sharding import PartitionSpec as P

PIVOT = 512


def outer_product(matrix, others):
    return lax.dot_general(
        matrix,
        others,
        (((1,), (1,)), ((), ())),
        precision=lax.Precision.HIGHEST,
        preferred_element_type=jnp.float32,
    )


def plain_product(matrix, others):
    return jnp.dot(
        matrix, others, precision=lax.Precision.HIGHEST, preferred_element_type=jnp.float32
    )


def body(pivot_block, pivot_tangent, panel_block, panel_tangent, strip_block, strip_tangent):
    row_index = lax.axis_index("row")
    col_index = lax.axis_index("col")
    pivot_rows_local = pivot_block.shape[0]
    pivot_cols_local = pivot_block.shape[1]
    tile_rows = strip_block.shape[1] // lax.axis_size("row")
    stacked = jnp.stack([pivot_block, pivot_tangent])
    halfway = lax.all_gather(stacked, "col", axis=2, tiled=True)
    whole_pivot = lax.all_gather(halfway, "row", axis=1, tiled=True)
    pivot_factor = jnp.linalg.cholesky(whole_pivot[0])
    identity = jnp.eye(PIVOT, dtype=jnp.float32)
    inverse = lax.linalg.triangular_solve(pivot_factor, identity, left_side=True, lower=True)
    mixed = outer_product(plain_product(inverse, whole_pivot[1]), inverse)
    halved = jnp.tril(mixed, -1) + 0.5 * jnp.diag(jnp.diag(mixed))
    pivot_change = plain_product(pivot_factor, halved)
    transposed_inverse = inverse.T
    panel_cols_local = panel_block.shape[1]
    panel_whole = lax.all_gather(jnp.stack([panel_block, panel_tangent]), "col", axis=2, tiled=True)
    panel_factor = plain_product(panel_whole[0], transposed_inverse)
    panel_change = plain_product(
        panel_whole[1] - outer_product(panel_factor, pivot_change), transposed_inverse
    )
    local_rows = panel_block.shape[0]
    own_rows = lax.dynamic_slice_in_dim(
        jnp.stack([panel_factor, panel_change]), col_index * tile_rows, tile_rows, 1
    )
    stacked_panel = jnp.concatenate([panel_factor, panel_change], 0)
    pieces = lax.all_gather(own_rows, "row", axis=1, tiled=True)
    product = outer_product(stacked_panel, pieces[0])
    second_term = outer_product(panel_factor, pieces[1])
    updates = jnp.stack([product[:local_rows], product[local_rows:] + second_term])
    strip_updated = strip_block - updates[0]
    strip_changed = strip_tangent - updates[1]
    corner = (row_index * pivot_rows_local, col_index * pivot_cols_local)
    factor_block = lax.dynamic_slice(pivot_factor, corner, (pivot_rows_local, pivot_cols_local))
    change_block = lax.dynamic_slice(pivot_change, corner, (pivot_rows_local, pivot_cols_local))
    panel_out = lax.dynamic_slice_in_dim(
        panel_factor, col_index * panel_cols_local, panel_cols_local, 1
    )
    panel_change_out = lax.dynamic_slice_in_dim(
        panel_change, col_index * panel_cols_local, panel_cols_local, 1
    )
    return (factor_block, change_block, panel_out, panel_change_out, strip_updated, strip_changed)


def solution(mesh):
    placed = (
        P("row", "col"),
        P("row", "col"),
        P("row", "col"),
        P("row", "col"),
        P("row", "col"),
        P("row", "col"),
    )
    return jax.shard_map(
        body,
        mesh=mesh,
        in_specs=placed,
        out_specs=(
            P("row", "col"),
            P("row", "col"),
            P("row", "col"),
            P("row", "col"),
            P("row", "col"),
            P("row", "col"),
        ),
        check_vma=False,
    )
```

profile of v0, /device:TPU:1, one launch (start us, length us, event | category | flops | bytes accessed | tf_op | source)
XLA Modules:
  0.0 382.7 jit_solution(3954354123918194901)
XLA Ops:
  7.2 0.7 pad_maximum_fusion.2
  7.9 9.4 %all_gather.12 = f32[2,8,512]{2,0,1:T(2,128)} all-gather(f32[2,8,128]{2,0,1:T(2,128)S(1)} %copy.18), channel_id=1, replica_groups=mesh['row'=64,'col'=4] {'col'}, dimensions={2}, use_global_device_ids=true | all-gather | bytes 40960 | tf_op jit(solution)/shard_map/all_gather | solution.py:32
  17.4 2.3 pad_maximum_fusion.1
  19.7 0.8 iota_compare_fusion
  20.5 0.1 fusion.24
  20.7 77.1 %all-gather.4.cloned.1.call-done = f32[2,512,512]{2,0,1:T(2,128)} async-done(((f32[2,8,512]{2,0,1:T(2,128)}), f32[2,512,512]{2,0,1:T(2,128)}) %all-gather.4.cloned.1.call-update) | async-done | bytes 2097168 | tf_op jit(solution)/shard_map/all_gather | solution.py:33
  97.8 5.0 %fusion.59 = (f32[1,512,512]{2,0,1:T(1,128)}, f32[1,512,512]{2,0,1:T(1,128)S(1)}) fusion(f32[2,512,512]{2,0,1:T(2,128)} %all-gather.4.cloned.1.call-done), kind=kLoop, calls=%fused_computation.111 | loop fusion | bytes 4194304 | tf_op jit(solution)/shard_map/slice | solution.py:37
  102.7 1.5 copy.22
  104.2 0.2 fusion.9
  104.5 1.0 copy-done.6
  105.4 11.7 %cholesky.104 = f32[128,128]{1,0:T(8,128)S(1)} custom-call(f32[128,128]{1,0:T(8,128)S(1)} %cholesky.266), custom_call_target="Cholesky" | custom-call | tf_op jit(solution)/shard_map/jit(cholesky)/cholesky | solution.py:34
  117.2 9.8 %custom-call.30 = f32[1,128,128]{1,2,0:T(8,128)S(1)} custom-call(f32[1,128,128]{2,1,0:T(8,128)S(1)} %get-tuple-element.37), custom_call_target="InvertDiagBlocksLowerTriangular" | custom-call | tf_op jit(solution)/shard_map/jit(cholesky)/cholesky | solution.py:34
  127.0 0.1 cholesky.224
  127.1 1.2 constant_dynamic-update-slice_fusion
  128.4 1.3 convolution_subtract_fusion.3
  129.7 11.7 %cholesky.217 = f32[128,128]{1,0:T(8,128)S(1)} custom-call(f32[128,128]{1,0:T(8,128)S(1)} %cholesky.270), custom_call_target="Cholesky" | custom-call | tf_op jit(solution)/shard_map/jit(cholesky)/cholesky | solution.py:34
  141.4 10.0 %custom-call.31 = f32[1,128,128]{1,2,0:T(8,128)S(1)} custom-call(f32[1,128,128]{2,1,0:T(8,128)S(1)} %get-tuple-element.34), custom_call_target="InvertDiagBlocksLowerTriangular" | custom-call | tf_op jit(solution)/shard_map/jit(cholesky)/cholesky | solution.py:34
  151.4 0.3 convolution_dynamic-update-slice_fusion
  151.7 1.3 convolution_subtract_fusion.4
  153.0 11.7 %cholesky.238 = f32[128,128]{1,0:T(8,128)S(1)} custom-call(f32[128,128]{1,0:T(8,128)S(1)} %cholesky.275), custom_call_target="Cholesky" | custom-call | tf_op jit(solution)/shard_map/jit(cholesky)/cholesky | solution.py:34
  164.8 9.8 %custom-call.32 = f32[1,128,128]{1,2,0:T(8,128)S(1)} custom-call(f32[1,128,128]{2,1,0:T(8,128)S(1)} %get-tuple-element.31), custom_call_target="InvertDiagBlocksLowerTriangular" | custom-call | tf_op jit(solution)/shard_map/jit(cholesky)/cholesky | solution.py:34
  174.6 0.2 convolution_dynamic-update-slice_fusion.1
  174.8 1.2 convolution_subtract_fusion.5
  176.0 11.7 %cholesky.255 = f32[128,128]{1,0:T(8,128)S(1)} custom-call(f32[128,128]{1,0:T(8,128)S(1)} %convolution_subtract_fusion.5), custom_call_target="Cholesky" | custom-call | tf_op jit(solution)/shard_map/jit(cholesky)/cholesky | solution.py:34
  187.7 0.6 compare_reduce_fusion.2
  189.7 0.6 compare_reduce_fusion.1
  191.0 0.6 compare_reduce_fusion
  192.3 1.2 fusion.18
  193.5 14.1 %while.1 = (s32[]{:T(128)}, f32[512,512]{1,0:T(8,128)}, s32[4,2]{0,1:T(2,128)S(1)}, f32[4,128,128]{2,1,0:T(8,128)}, s32[]{:T(128)}) while((s32[]{:T(128)}, f32[512,512]{1,0:T(8,128)}, s32[4,2]{0,1:T(2,128)S(1)}, f32[4,128,128]{2,1,0:T(8,128)}, s32[]{:T(128)}) %tuple.33), condition=%wide.while_cond, body=%wide.while_body.sunk | while | flops 2 | bytes 132205 | solution.py:36
  193.5 0.1 constant_dynamic-slice_fusion.4
  193.6 0.6 fusion.72
  194.2 2.9 bitcast_dynamic-update-slice_fusion.2
  197.2 0.5 fusion.72
  197.7 2.9 bitcast_dynamic-update-slice_fusion.2
  200.7 0.5 fusion.72
  201.3 2.9 bitcast_dynamic-update-slice_fusion.2
  204.3 0.5 fusion.72
  204.8 2.9 bitcast_dynamic-update-slice_fusion.2
  207.6 40.5 %custom-call.33 = f32[4,128,128]{1,2,0:T(8,128)S(1)} custom-call(f32[4,128,128]{2,1,0:T(8,128)} %get-tuple-element.13), custom_call_target="InvertDiagBlocksLowerTriangular" | custom-call | tf_op jit(solution)/shard_map/triangular_solve | solution.py:36
  248.2 1.2 fusion.33
  249.4 1.2 convolution_subtract_fusion.1
  250.6 1.4 fusion.45
  252.0 1.4 convolution_subtract_fusion
  253.4 1.3 fusion.43
  254.7 1.7 convolution_subtract_fusion.2
  256.4 1.3 fusion.42
  257.7 1.8 fusion.10
  259.5 1.9 fusion.57
  261.4 4.7 %gather_fusion = f32[512]{0:T(512)S(1)} fusion(f32[512,512]{1,0:T(8,128)S(1)} %fusion.57, s32[512]{0:T(512)S(1)} %bitcast.82), kind=kCustom, calls=%fused_computation | custom fusion | bytes 8192 | tf_op jit(solution)/shard_map/jit(_diag)/jit(diagonal)/cond/branch_0_fun/gather | solution.py:38
  266.1 3.0 fusion.13
  269.1 5.2 %fusion.8 = f32[1024,512]{1,0:T(8,128)S(1)} fusion(f32[2,1024,512]{2,1,0:T(8,128)} %all-gather.6.cloned.1.call-done, f32[128,512]{1,0:T(8,128)S(1)} %fusion.42, f32[128,512]{1,0:T(8,128)S(1)} %fusion.43, f32[128,512]{1,0:T(8,128)S(1)} %fusion.45, f32[128,512]{1,0:T(8,128)S(1)} %fusion.33), kind=kOutput, calls=%fused_computation.16 | convolution fusion | flops 3222011904 | bytes 5242880 | tf_op jit(solution)/shard_map/dot_general | solution.py:20
  274.3 3.5 fusion.60
  277.8 3.7 fusion.6
  281.6 1.3 copy-done
  282.9 0.6 fusion.51
  283.5 1.3 dynamic_slice.15
  284.8 1.3 dynamic_slice.16
  286.1 0.9 constant_dynamic-slice_fusion.2
  287.0 1.9 constant_dynamic-slice_fusion.1
  288.8 69.8 %all-gather.8.cloned.1.call-done = f32[2,512,512]{2,1,0:T(8,128)} async-done(((f32[2,8,512]{2,1,0:T(8,128)}), f32[2,512,512]{2,1,0:T(8,128)}) %all-gather.8.cloned.1.call-update) | async-done | bytes 2097168 | tf_op jit(solution)/shard_map/all_gather | solution.py:52
  358.6 9.3 %fusion = f32[2048,512]{1,0:T(8,128)S(1)} fusion(f32[1024,512]{1,0:T(8,128)} %copy-done, f32[1024,512]{1,0:T(8,128)S(1)} %fusion.8, f32[2,512,512]{2,1,0:T(8,128)} %all-gather.8.cloned.1.call-done), kind=kOutput, calls=%fused_computation.3 | convolution fusion | flops 6443499520 | bytes 9437184 | tf_op jit(solution)/shard_map/dot_general | solution.py:10
  367.9 1.8 slice_subtract_fusion
  369.7 1.1 copy-done.9
  370.8 5.1 %fusion.4 = f32[1024,512]{1,0:T(8,128)} fusion(f32[1024,512]{1,0:T(8,128)S(1)} %copy-done.9, f32[2048,512]{1,0:T(8,128)S(1)} %fusion, f32[1024,512]{1,0:T(8,128)S(1)} %fusion.8, f32[2,512,512]{2,1,0:T(8,128)S(1)} %copy-done.8), kind=kOutput, calls=%fused_computation.10 | convolution fusion | flops 3222274048 | bytes 9437184 | tf_op jit(solution)/shard_map/dot_general | solution.py:10
  (42 shorter events, 0.7 us)
Async XLA Ops:
  7.2 90.6 %all-gather.4.cloned.1.call-start = ((), (), s32[]{:S(2)}) async-start(), calls=%async_computation | async-start | bytes 2129920 | tf_op jit(solution)/shard_map/all_gather | solution.py:33
  17.3 251.8 %all-gather.6.cloned.1.call-start = ((), (), s32[]{:S(2)}) async-start(), calls=%async_computation.1 | async-start | bytes 5242880 | tf_op jit(solution)/shard_map/all_gather | solution.py:42
  19.7 338.9 %all-gather.8.cloned.1.call-start = ((), (), s32[]{:S(2)}) async-start(), calls=%async_computation.2 | async-start | bytes 2129920 | tf_op jit(solution)/shard_map/all_gather | solution.py:52
  20.6 228.7 %copy-start.5 = (f32[512,512]{1,0:T(8,128)}, f32[512,512]{1,0:T(8,128)S(1)}, u32[]{:S(2)}) copy-start(f32[512,512]{1,0:T(8,128)S(1)} %fusion.24) | copy-start | bytes 3145732
  104.5 1.0 copy-start.6
  193.5 72.6 %copy-start.2 = (f32[512,512]{1,0:T(8,128)}, f32[512,512]{1,0:T(8,128)S(1)}, u32[]{:S(2)}) copy-start(f32[512,512]{1,0:T(8,128)S(1)} %get-tuple-element.23) | copy-start | bytes 3145732
  248.2 1.2 copy-start.10
  250.6 7.1 %copy-start.4 = (f32[1,512,512]{2,0,1:T(1,128)S(1)}, f32[1,512,512]{2,0,1:T(1,128)}, u32[]{:S(2)}) copy-start(f32[1,512,512]{2,0,1:T(1,128)} %get-tuple-element.26) | copy-start | bytes 3145732
  269.1 5.2 %copy-start.1 = (f32[512,512]{1,0:T(8,128)S(1)}, f32[512,512]{1,0:T(8,128)}, u32[]{:S(2)}) copy-start(f32[512,512]{1,0:T(8,128)} %fusion.13) | copy-start | bytes 3145732
  274.3 3.5 copy-start.3
  281.6 1.3 copy-start
  358.6 9.3 %copy-start.7 = (f32[1024,512]{1,0:T(8,128)S(1)}, f32[1024,512]{1,0:T(8,128)}, u32[]{:S(2)}) copy-start(f32[1024,512]{1,0:T(8,128)} %param.10) | copy-start | bytes 6291460
  367.9 1.9 copy-start.8
  367.9 3.0 copy-start.9
Sparse Core Ops, SparseCore 0:
  17.4 80.2 all-gather.3
  99.6 51.2 all-gather.5
  283.7 74.8 all-gather.7
where the time goes:
time: 386 us; the launch traced here: 383 us
  waiting for transfers between devices  147 us (38%)
  other arithmetic  127 us (33%)
  matrix products  48.4 us (13%)
  local copies, waits for them, and re-layouts  34.2 us (9%)
  between operations  17 us (4%)
  blocking collectives  9.36 us (2%)
    another operation x14, other arithmetic, body(): pivot_factor = jnp.linalg.cholesky(whole_pivot[0])  78.5 us
    all_gather x1, waiting for transfers between devices, body(): whole_pivot = lax.all_gather(halfway, 'row', axis=1, tiled=True)  77.1 us
    all_gather x1, waiting for transfers between devices, body(): pieces = lax.all_gather(own_rows, 'row', axis=1, tiled=True)  69.8 us
    another operation x3, other arithmetic, body(): lax.linalg.triangular_solve(pivot_factor, identity, left_side=True, lower...  41.7 us
    dot_general x4, matrix products, outer_product(): lax.dot_general(matrix, others, (((1,), (1,)), ((), ())), precision=lax.P...  19.7 us
    another operation x12, local copies, waits for them, and re-layouts  14.1 us
    dot_general x4, matrix products, plain_product(): jnp.dot(matrix, others, precision=lax.Precision.HIGHEST, preferred_elemen...  13.8 us
    another operation x7, matrix products, body(): lax.linalg.triangular_solve(pivot_factor, identity, left_side=True, lower...  9.4 us
  transfers between devices with their start and end apart: 3, of which 2 were waited for; matrix products, arithmetic and copies ran while one was open for 46% of the time, Pallas kernels for 0%

commit v1 on v0

--- a/solution.py
+++ b/solution.py
@@ -49,7 +49,10 @@
         jnp.stack([panel_factor, panel_change]), col_index * tile_rows, tile_rows, 1
     )
     stacked_panel = jnp.concatenate([panel_factor, panel_change], 0)
-    pieces = lax.all_gather(own_rows, "row", axis=1, tiled=True)
+    leaves = []
+    for _ in range(lax.axis_size("row")):
+        leaves.append(own_rows)
+    pieces = jnp.concatenate(lax.all_to_all(jnp.stack(leaves), "row", 0, 0), axis=1)
     product = outer_product(stacked_panel, pieces[0])
     second_term = outer_product(panel_factor, pieces[1])
     updates = jnp.stack([product[:local_rows], product[local_rows:] + second_term])

time: 386 us -> 371 us (0.961)
  waiting for transfers between devices: 147 us -> 123 us
  starting transfers between devices: 0.12 us -> 6.93 us
    all_gather x1 -> x0, waiting for transfers between devices: 69.8 us -> none  [body(): pieces = lax.all_gather(own_rows, 'row', axis=1, tiled=True)]
    all_to_all x0 -> x1, waiting for transfers between devices: none -> 45.9 us  [body(): lax.all_to_all(jnp.stack(leaves), 'row', 0, 0)]
    all_to_all x0 -> x1, starting transfers between devices: none -> 6.85 us  [body(): lax.all_to_all(jnp.stack(leaves), 'row', 0, 0)]
    another operation x12 -> x13, local copies, waits for them, and re-layouts: 14.1 us -> 15.7 us
  transfers between devices with their start and end apart: 3 -> 3, of which waited for: 2 -> 2; matrix products, arithmetic and copies ran while one was open for 46% -> 48% of each run, Pallas kernels for 0% -> 0%
where the time goes in v1:
time: 371 us; the launch traced here: 367 us
  other arithmetic  126 us (34%)
  waiting for transfers between devices  123 us (33%)
  matrix products  49.7 us (13%)
  local copies, waits for them, and re-layouts  34.5 us (9%)
  between operations  17.3 us (5%)
  blocking collectives  9.36 us (3%)
  starting transfers between devices  6.93 us (2%)
    another operation x14, other arithmetic, body(): pivot_factor = jnp.linalg.cholesky(whole_pivot[0])  78.5 us
    all_gather x1, waiting for transfers between devices, body(): whole_pivot = lax.all_gather(halfway, 'row', axis=1, tiled=True)  77.1 us
    all_to_all x1, waiting for transfers between devices, body(): lax.all_to_all(jnp.stack(leaves), 'row', 0, 0)  45.9 us
    another operation x3, other arithmetic, body(): lax.linalg.triangular_solve(pivot_factor, identity, left_side=True, lower...  41.7 us
    dot_general x4, matrix products, outer_product(): lax.dot_general(matrix, others, (((1,), (1,)), ((), ())), precision=lax.P...  21 us
    another operation x12, local copies, waits for them, and re-layouts  14.1 us
    dot_general x4, matrix products, plain_product(): jnp.dot(matrix, others, precision=lax.Precision.HIGHEST, preferred_elemen...  13.8 us
    another operation x7, matrix products, body(): lax.linalg.triangular_solve(pivot_factor, identity, left_side=True, lower...  9.39 us
  transfers between devices with their start and end apart: 3, of which 2 were waited for; matrix products, arithmetic and copies ran while one was open for 48% of the time, Pallas kernels for 0%

profile of v1, /device:TPU:1, one launch (start us, length us, event | category | flops | bytes accessed | tf_op | source)
XLA Modules:
  0.0 367.1 jit_solution(14787019634981765317)
XLA Ops:
  7.2 0.7 pad_maximum_fusion.2
  7.9 9.4 %all_gather.9 = f32[2,8,512]{2,0,1:T(2,128)} all-gather(f32[2,8,128]{2,0,1:T(2,128)S(1)} %copy.18), channel_id=1, replica_groups=mesh['row'=64,'col'=4] {'col'}, dimensions={2}, use_global_device_ids=true | all-gather | bytes 40960 | tf_op jit(solution)/shard_map/all_gather | solution.py:32
  17.4 2.3 pad_maximum_fusion.1
  19.7 0.8 iota_compare_fusion
  20.5 0.1 fusion.24
  20.6 77.1 %all-gather.3.cloned.1.call-done = f32[2,512,512]{2,0,1:T(2,128)} async-done(((f32[2,8,512]{2,0,1:T(2,128)}), f32[2,512,512]{2,0,1:T(2,128)}) %all-gather.3.cloned.1.call-update) | async-done | bytes 2097168 | tf_op jit(solution)/shard_map/all_gather | solution.py:33
  97.8 5.0 %fusion.59 = (f32[1,512,512]{2,0,1:T(1,128)}, f32[1,512,512]{2,0,1:T(1,128)S(1)}) fusion(f32[2,512,512]{2,0,1:T(2,128)} %all-gather.3.cloned.1.call-done), kind=kLoop, calls=%fused_computation.111 | loop fusion | bytes 4194304 | tf_op jit(solution)/shard_map/slice | solution.py:37
  102.7 1.5 copy.22
  104.2 0.2 fusion.9
  104.5 1.0 copy-done.6
  105.4 11.7 %cholesky.104 = f32[128,128]{1,0:T(8,128)S(1)} custom-call(f32[128,128]{1,0:T(8,128)S(1)} %cholesky.266), custom_call_target="Cholesky" | custom-call | tf_op jit(solution)/shard_map/jit(cholesky)/cholesky | solution.py:34
  117.2 9.8 %custom-call.30 = f32[1,128,128]{1,2,0:T(8,128)S(1)} custom-call(f32[1,128,128]{2,1,0:T(8,128)S(1)} %get-tuple-element.37), custom_call_target="InvertDiagBlocksLowerTriangular" | custom-call | tf_op jit(solution)/shard_map/jit(cholesky)/cholesky | solution.py:34
  127.0 0.1 cholesky.224
  127.1 1.2 constant_dynamic-update-slice_fusion
  128.4 1.3 convolution_subtract_fusion.3
  129.7 11.7 %cholesky.217 = f32[128,128]{1,0:T(8,128)S(1)} custom-call(f32[128,128]{1,0:T(8,128)S(1)} %cholesky.270), custom_call_target="Cholesky" | custom-call | tf_op jit(solution)/shard_map/jit(cholesky)/cholesky | solution.py:34
  141.4 10.0 %custom-call.31 = f32[1,128,128]{1,2,0:T(8,128)S(1)} custom-call(f32[1,128,128]{2,1,0:T(8,128)S(1)} %get-tuple-element.34), custom_call_target="InvertDiagBlocksLowerTriangular" | custom-call | tf_op jit(solution)/shard_map/jit(cholesky)/cholesky | solution.py:34
  151.4 0.3 convolution_dynamic-update-slice_fusion
  151.7 1.3 convolution_subtract_fusion.4
  153.0 11.7 %cholesky.238 = f32[128,128]{1,0:T(8,128)S(1)} custom-call(f32[128,128]{1,0:T(8,128)S(1)} %cholesky.275), custom_call_target="Cholesky" | custom-call | tf_op jit(solution)/shard_map/jit(cholesky)/cholesky | solution.py:34
  164.8 9.8 %custom-call.32 = f32[1,128,128]{1,2,0:T(8,128)S(1)} custom-call(f32[1,128,128]{2,1,0:T(8,128)S(1)} %get-tuple-element.31), custom_call_target="InvertDiagBlocksLowerTriangular" | custom-call | tf_op jit(solution)/shard_map/jit(cholesky)/cholesky | solution.py:34
  174.6 0.2 convolution_dynamic-update-slice_fusion.1
  174.8 1.2 convolution_subtract_fusion.5
  176.0 11.7 %cholesky.255 = f32[128,128]{1,0:T(8,128)S(1)} custom-call(f32[128,128]{1,0:T(8,128)S(1)} %convolution_subtract_fusion.5), custom_call_target="Cholesky" | custom-call | tf_op jit(solution)/shard_map/jit(cholesky)/cholesky | solution.py:34
  187.7 0.6 compare_reduce_fusion.2
  189.7 0.6 compare_reduce_fusion.1
  191.0 0.6 compare_reduce_fusion
  192.3 1.2 fusion.18
  193.5 14.1 %while.1 = (s32[]{:T(128)}, f32[512,512]{1,0:T(8,128)}, s32[4,2]{0,1:T(2,128)S(1)}, f32[4,128,128]{2,1,0:T(8,128)}, s32[]{:T(128)}) while((s32[]{:T(128)}, f32[512,512]{1,0:T(8,128)}, s32[4,2]{0,1:T(2,128)S(1)}, f32[4,128,128]{2,1,0:T(8,128)}, s32[]{:T(128)}) %tuple.33), condition=%wide.while_cond, body=%wide.while_body.sunk | while | flops 2 | bytes 132205 | solution.py:36
  193.5 0.1 constant_dynamic-slice_fusion.4
  193.6 0.6 fusion.72
  194.2 2.9 bitcast_dynamic-update-slice_fusion.2
  197.2 0.5 fusion.72
  197.7 2.9 bitcast_dynamic-update-slice_fusion.2
  200.7 0.5 fusion.72
  201.3 2.9 bitcast_dynamic-update-slice_fusion.2
  204.3 0.5 fusion.72
  204.8 2.9 bitcast_dynamic-update-slice_fusion.2
  207.6 40.5 %custom-call.33 = f32[4,128,128]{1,2,0:T(8,128)S(1)} custom-call(f32[4,128,128]{2,1,0:T(8,128)} %get-tuple-element.13), custom_call_target="InvertDiagBlocksLowerTriangular" | custom-call | tf_op jit(solution)/shard_map/triangular_solve | solution.py:36
  248.2 1.2 fusion.33
  249.4 1.2 convolution_subtract_fusion.1
  250.6 1.3 fusion.45
  252.0 1.4 convolution_subtract_fusion
  253.4 1.3 fusion.43
  254.7 1.7 convolution_subtract_fusion.2
  256.4 1.3 fusion.42
  257.7 1.8 fusion.10
  259.5 1.9 fusion.57
  261.4 4.7 %gather_fusion = f32[512]{0:T(512)S(1)} fusion(f32[512,512]{1,0:T(8,128)S(1)} %fusion.57, s32[512]{0:T(512)S(1)} %bitcast.83), kind=kCustom, calls=%fused_computation | custom fusion | bytes 8192 | tf_op jit(solution)/shard_map/jit(_diag)/jit(diagonal)/cond/branch_0_fun/gather | solution.py:38
  266.1 3.1 fusion.13
  269.2 5.2 %fusion.8 = f32[1024,512]{1,0:T(8,128)S(1)} fusion(f32[2,1024,512]{2,1,0:T(8,128)} %all-gather.5.cloned.1.call-done, f32[128,512]{1,0:T(8,128)S(1)} %fusion.42, f32[128,512]{1,0:T(8,128)S(1)} %fusion.43, f32[128,512]{1,0:T(8,128)S(1)} %fusion.45, f32[128,512]{1,0:T(8,128)S(1)} %fusion.33), kind=kOutput, calls=%fused_computation.16 | convolution fusion | flops 3222011904 | bytes 5242880 | tf_op jit(solution)/shard_map/dot_general | solution.py:20
  274.4 3.5 fusion.60
  277.9 3.7 %fusion.6 = f32[1024,512]{1,0:T(8,128)S(1)} fusion(f32[1024,512]{1,0:T(8,128)S(1)} %fusion.60, f32[2,1024,512]{2,1,0:T(8,128)S(1)} %copy-done.3, f32[128,512]{1,0:T(8,128)S(1)} %fusion.42, f32[128,512]{1,0:T(8,128)S(1)} %fusion.43, f32[128,512]{1,0:T(8,128)S(1)} %fusion.45, f32[128,512]{1,0:T(8,128)S(1)} %fusion.33), kind=kOutput, calls=%fused_computation.14 | convolution fusion | flops 3222536192 | bytes 7340032 | tf_op jit(solution)/shard_map/dot_general | solution.py:20
  281.6 1.3 copy-done
  282.9 1.6 stack.29
  284.5 6.8 %all-to-all-start = ((f32[64,2,8,512]{3,2,1,0:T(8,128)}), f32[64,2,8,512]{3,2,1,0:T(8,128)}, u32[]{:S(2)}, u32[]{:S(2)}) async-start(f32[64,2,8,512]{3,2,1,0:T(8,128)} %stack.29), calls=%async_computation | async-start | bytes 4194304 | tf_op jit(solution)/shard_map/all_to_all | solution.py:55
  291.4 1.3 dynamic_slice.15
  292.7 1.3 dynamic_slice.16
  293.9 0.9 constant_dynamic-slice_fusion.2
  294.8 1.9 constant_dynamic-slice_fusion.1
  296.6 45.9 %all-to-all-done = f32[64,2,8,512]{3,2,1,0:T(8,128)} async-done(((f32[64,2,8,512]{3,2,1,0:T(8,128)}), f32[64,2,8,512]{3,2,1,0:T(8,128)}, u32[]{:S(2)}, u32[]{:S(2)}) %all-to-all-start) | async-done | bytes 2097184 | tf_op jit(solution)/shard_map/all_to_all | solution.py:55
  342.5 9.3 %fusion = f32[2048,512]{1,0:T(8,128)S(1)} fusion(f32[1024,512]{1,0:T(8,128)} %copy-done, f32[1024,512]{1,0:T(8,128)S(1)} %fusion.8, f32[2,64,8,512]{3,2,0,1:T(8,128)} %bitcast.21), kind=kOutput, calls=%fused_computation.3 | convolution fusion | flops 6443499520 | bytes 9437184 | tf_op jit(solution)/shard_map/dot_general | solution.py:10
  351.8 6.4 %fusion.4 = f32[1024,512]{1,0:T(8,128)} fusion(f32[1024,512]{1,0:T(8,128)S(1)} %copy-done.8, f32[2048,512]{1,0:T(8,128)S(1)} %fusion, f32[1024,512]{1,0:T(8,128)S(1)} %fusion.8, f32[2,64,8,512]{3,2,0,1:T(8,128)} %bitcast.21), kind=kOutput, calls=%fused_computation.10 | convolution fusion | flops 3222274048 | bytes 9437184 | tf_op jit(solution)/shard_map/dot_general | solution.py:10
  358.2 1.8 slice_subtract_fusion
  (40 shorter events, 0.6 us)
Async XLA Ops:
  7.2 90.6 %all-gather.3.cloned.1.call-start = ((), (), s32[]{:S(2)}) async-start(), calls=%async_computation.1 | async-start | bytes 2129920 | tf_op jit(solution)/shard_map/all_gather | solution.py:33
  17.3 251.9 %all-gather.5.cloned.1.call-start = ((), (), s32[]{:S(2)}) async-start(), calls=%async_computation.2 | async-start | bytes 5242880 | tf_op jit(solution)/shard_map/all_gather | solution.py:42
  20.6 228.8 %copy-start.5 = (f32[512,512]{1,0:T(8,128)}, f32[512,512]{1,0:T(8,128)S(1)}, u32[]{:S(2)}) copy-start(f32[512,512]{1,0:T(8,128)S(1)} %fusion.24) | copy-start | bytes 3145732
  104.5 1.0 copy-start.6
  193.5 72.6 %copy-start.2 = (f32[512,512]{1,0:T(8,128)}, f32[512,512]{1,0:T(8,128)S(1)}, u32[]{:S(2)}) copy-start(f32[512,512]{1,0:T(8,128)S(1)} %get-tuple-element.23) | copy-start | bytes 3145732
  248.1 1.2 copy-start.9
  250.6 7.1 %copy-start.4 = (f32[1,512,512]{2,0,1:T(1,128)S(1)}, f32[1,512,512]{2,0,1:T(1,128)}, u32[]{:S(2)}) copy-start(f32[1,512,512]{2,0,1:T(1,128)} %get-tuple-element.26) | copy-start | bytes 3145732
  269.2 5.2 %copy-start.1 = (f32[512,512]{1,0:T(8,128)S(1)}, f32[512,512]{1,0:T(8,128)}, u32[]{:S(2)}) copy-start(f32[512,512]{1,0:T(8,128)} %fusion.13) | copy-start | bytes 3145732
  274.3 3.5 copy-start.3
  281.6 1.3 copy-start
  284.5 58.0 %all-to-all-start = ((f32[64,2,8,512]{3,2,1,0:T(8,128)}), f32[64,2,8,512]{3,2,1,0:T(8,128)}, u32[]{:S(2)}, u32[]{:S(2)}) async-start(f32[64,2,8,512]{3,2,1,0:T(8,128)} %stack.29), calls=%async_computation | async-start | bytes 4194304 | tf_op jit(solution)/shard_map/all_to_all | solution.py:55
  342.5 9.3 %copy-start.8 = (f32[1024,512]{1,0:T(8,128)S(1)}, f32[1024,512]{1,0:T(8,128)}, u32[]{:S(2)}) copy-start(f32[1024,512]{1,0:T(8,128)} %param.11) | copy-start | bytes 6291460
  351.8 6.4 %copy-start.7 = (f32[1024,512]{1,0:T(8,128)S(1)}, f32[1024,512]{1,0:T(8,128)}, u32[]{:S(2)}) copy-start(f32[1024,512]{1,0:T(8,128)} %param.10) | copy-start | bytes 6291460
Sparse Core Ops, SparseCore 0:
  17.4 80.2 all-gather.2
  99.6 51.2 all-gather.4
